TPU v7x, 512 devices: a whole 4x8x8 slice. The times are simulated.
512 devices in a mesh: ctx: 64 (over x, z_lo, y), head: 8 (over z_hi, core).
Axes of the slice: x: 4, y: 8, z: 8 (z_hi: 4, z_lo: 2; z = z_hi * 2 + z_lo), core: 2. Of those that a mesh axis runs over, the one named last changes fastest.
Arguments:
- queries: bfloat16 [8192, 4096], P(('ctx', 'head')), may hold values from -30 to 30
- keys: bfloat16 [8192, 1024], P(('ctx', 'head')), may hold values from -6 to 6
- values: bfloat16 [8192, 1024], P(('ctx', 'head')), may hold values from -6 to 6
- outputs: bfloat16 [8192, 4096], P(('ctx', 'head')), may hold values from -6 to 6
- output_gradient: bfloat16 [8192, 4096], P(('ctx', 'head')), may hold values from -6 to 6
- importance: int32 [8192], P('ctx'), may hold values from 0 to 8
- span_order: int32 [128], replicated, may hold values from 0 to 127, each once
Outputs:
- query_grad: bfloat16 [8192, 4096], P(('ctx', 'head'))
- key_gradient: bfloat16 [8192, 1024], P(('ctx', 'head'))
- value_gradient: bfloat16 [8192, 1024], P(('ctx', 'head'))
All inputs are finite; a program needn't handle non-finite values.
Results may differ from a plain program's by a relative error of at most 0.0049.
Values may be sent and summed in bfloat16 or wider, within the bound.
A program may use at most 64 MiB of HBM per device.

v0:
```python
import math
import jax
import jax.numpy as jnp
from jax import lax
from jax.sharding import PartitionSpec as P

QUERY_HEADS = 32
KEY_VALUE_HEADS = 8
HEAD_WIDTH = 128
CH = 64
very_low = -1e30


def shifted(array, axis, by):
    size = lax.axis_size(axis)
    return lax.ppermute(array, axis, [(i, (i + by) % size) for i in range(size)])


def key_positions(span_order):
    span_count = span_order.shape[0]
    token_index = jnp.arange(span_count * CH, dtype=jnp.int32)
    span_index = token_index // CH
    matches = span_index[:, None] == jnp.arange(span_count, dtype=jnp.int32)[None, :]
    return jnp.sum(jnp.where(matches, span_order[None, :], 0), axis=1) * CH + token_index % CH


def block_split(length):
    if length > 512 and length % 512 == 0:
        return (512, length // 512)
    return (length, 1)


def on_device(queries, keys, values, outputs, output_gradient, importance, span_order):
    query_loc, output_loc, grad_loc, key_loc, value_loc = (
        lax.all_to_all(queries, "head", split_axis=1, concat_axis=0, tiled=True),
        lax.all_to_all(outputs, "head", split_axis=1, concat_axis=0, tiled=True),
        lax.all_to_all(output_gradient, "head", split_axis=1, concat_axis=0, tiled=True),
        lax.all_to_all(keys, "head", split_axis=1, concat_axis=0, tiled=True),
        lax.all_to_all(values, "head", split_axis=1, concat_axis=0, tiled=True),
    )
    row_count = query_loc.shape[0]
    kv_local = key_loc.shape[1] // HEAD_WIDTH
    group_width = QUERY_HEADS // KEY_VALUE_HEADS
    score_scale = 1.0 / math.sqrt(HEAD_WIDTH)
    cycle_count = lax.axis_size("ctx")
    my_index = lax.axis_index("ctx")
    heads_of_queries = query_loc.reshape(row_count, kv_local, group_width, HEAD_WIDTH)
    gradient_heads = grad_loc.reshape(row_count, kv_local, group_width, HEAD_WIDTH)
    output_heads = output_loc.reshape(row_count, kv_local, group_width, HEAD_WIDTH)
    out_dot = jnp.sum(
        gradient_heads.astype(jnp.float32) * output_heads.astype(jnp.float32), axis=-1
    )
    all_positions = key_positions(span_order)
    query_pos = lax.dynamic_slice_in_dim(all_positions, my_index * row_count, row_count)
    token_gain = importance.astype(jnp.float32) * 0.25
    grad_scale = (token_gain * score_scale)[:, None, None, None]
    gain_wide = token_gain[:, None, None, None]

    def scores_of(key_block, key_pos):
        key_split = key_block.reshape(key_block.shape[0], kv_local, HEAD_WIDTH)
        raw_scores = (
            jnp.einsum(
                "rcgd,ncd->rcgn", heads_of_queries, key_split, preferred_element_type=jnp.float32
            )
            * score_scale
        )
        visible = key_pos[None, None, None, :] <= query_pos[:, None, None, None]
        return (key_split, raw_scores, visible)

    def stats_block(running, inputs):
        key_split, raw_scores, visible = scores_of(inputs[0], inputs[1])
        masked = jnp.where(visible, raw_scores, very_low)
        running_max = jnp.maximum(running[0], jnp.max(masked, axis=-1))
        denominator = running[1] * jnp.exp(running[0] - running_max) + jnp.sum(
            jnp.where(visible, jnp.exp(masked - running_max[..., None]), 0.0), axis=-1
        )
        return ((running_max, denominator), None)

    def grads_block(log_norm, key_block, value_block, key_pos):
        key_split, raw_scores, visible = scores_of(key_block, key_pos)
        value_split = value_block.reshape(value_block.shape[0], kv_local, HEAD_WIDTH)
        probs = jnp.where(visible, jnp.exp(raw_scores - log_norm[..., None]), 0.0)
        prob_grads = jnp.einsum(
            "rcgd,ncd->rcgn", gradient_heads, value_split, preferred_element_type=jnp.float32
        )
        score_grads = (probs * (prob_grads - out_dot[..., None]) * grad_scale).astype(jnp.bfloat16)
        weighted = (probs * gain_wide).astype(jnp.bfloat16)
        query_term = jnp.einsum(
            "rcgn,ncd->rcgd", score_grads, key_split, preferred_element_type=jnp.float32
        )
        key_term = jnp.einsum(
            "rcgn,rcgd->ncd", score_grads, heads_of_queries, preferred_element_type=jnp.float32
        )
        value_term = jnp.einsum(
            "rcgn,rcgd->ncd", weighted, gradient_heads, preferred_element_type=jnp.float32
        )
        length = key_block.shape[0]
        return (
            query_term,
            jnp.concatenate([key_term.reshape(length, -1), value_term.reshape(length, -1)], axis=1),
        )

    def grads_over(log_norm, query_start, key_portion, value_portion, offset):
        length = key_portion.shape[0]
        block_len, block_count = block_split(length)
        key_pos = lax.dynamic_slice_in_dim(all_positions, offset, length)

        def one_block(query_sum, inputs):
            query_term, pair_term = grads_block(log_norm, inputs[0], inputs[1], inputs[2])
            return (query_sum + query_term, pair_term)

        query_sum, pair_terms = lax.scan(
            one_block,
            query_start,
            (
                key_portion.reshape(block_count, block_len, -1),
                value_portion.reshape(block_count, block_len, -1),
                key_pos.reshape(block_count, block_len),
            ),
        )
        return (query_sum, pair_terms.reshape(length, -1))

    stats_start = (
        jnp.full((row_count, kv_local, group_width), very_low, jnp.float32),
        jnp.zeros((row_count, kv_local, group_width), jnp.float32),
    )
    query_zero = jnp.zeros((row_count, kv_local, group_width, HEAD_WIDTH), jnp.float32)
    pair_zero = jnp.zeros((row_count, 2 * kv_local * HEAD_WIDTH), jnp.float32)
    running = stats_start
    portion = lax.all_gather(key_loc, "ctx", axis=0, tiled=True)
    length = portion.shape[0]
    block_len, block_count = block_split(length)
    key_pos = all_positions
    running, unused = lax.scan(
        stats_block,
        running,
        (portion.reshape(block_count, block_len, -1), key_pos.reshape(block_count, block_len)),
    )
    running_max, denominator = running
    log_norm = running_max + jnp.log(denominator)

    def cycle_step(step, carry):
        key_block, value_block, pair_acc, query_sum = carry
        anchor = (my_index - step + cycle_count) % cycle_count
        offset = anchor * row_count
        query_sum, pair_terms = grads_over(log_norm, query_sum, key_block, value_block, offset)
        key_block, value_block = shifted((key_block, value_block), "ctx", 1)
        pair_acc = shifted(pair_acc + pair_terms, "ctx", 1)
        return (key_block, value_block, pair_acc, query_sum)

    unused_keys, unused_values, pair_share, query_sum = lax.fori_loop(
        0, cycle_count, cycle_step, (key_loc, value_loc, pair_zero, query_zero)
    )
    key_width = kv_local * HEAD_WIDTH
    query_part = query_sum.reshape(row_count, -1).astype(jnp.bfloat16)
    key_part = pair_share[:, :key_width].astype(jnp.bfloat16)
    value_part = pair_share[:, key_width:].astype(jnp.bfloat16)
    return (
        lax.all_to_all(query_part, "head", split_axis=0, concat_axis=1, tiled=True),
        lax.all_to_all(key_part, "head", split_axis=0, concat_axis=1, tiled=True),
        lax.all_to_all(value_part, "head", split_axis=0, concat_axis=1, tiled=True),
    )


def solution(mesh):
    in_specs = (
        P(("ctx", "head"), None),
        P(("ctx", "head"), None),
        P(("ctx", "head"), None),
        P(("ctx", "head"), None),
        P(("ctx", "head"), None),
        P("ctx"),
        P(),
    )
    out_specs = (P(("ctx", "head"), None), P(("ctx", "head"), None), P(("ctx", "head"), None))
    return jax.shard_map(
        on_device, mesh=mesh, in_specs=in_specs, out_specs=out_specs, check_vma=False
    )
```

profile of v0, /device:TPU:1, one launch (start us, length us, event | category | flops | bytes accessed | tf_op | source)
XLA Modules:
  0.0 1430.9 jit_solution(9999002778378512729)
XLA Ops:
  7.9 19.0 %all_to_all.137 = bf16[16,8,128]{2,0,1:T(8,128)(2,1)} all-to-all(bf16[16,8,128]{2,0,1:T(8,128)(2,1)S(1)} %copy_bitcast_fusion.6), channel_id=1, replica_groups=mesh['ctx'=64,'head'=8] {'head'}, dimensions={1} | all-to-all | bytes 65536 | tf_op jit(solution)/shard_map/all_to_all | solution.py:38
  28.5 4.0 all-to-all-start.2
  40.6 5.0 all-to-all-start.3
  47.2 7.1 all-to-all-done.3
  54.3 4.4 all-to-all-start.4
  60.3 7.5 all-to-all-done.4
  67.8 4.2 all-to-all-start.1
  72.5 207.1 %all-gather.2.cloned.1.call-done = bf16[8192,128]{1,0:T(8,128)(2,1)} async-done(((bf16[128,128]{1,0:T(8,128)(2,1)}), bf16[8192,128]{1,0:T(8,128)(2,1)}) %all-gather.2.cloned.1.call-update) | async-done | bytes 2097168 | tf_op jit(solution)/shard_map/all_gather | solution.py:130
  279.6 26.5 %while.46 = (s32[]{:T(128)}, f32[128,1,4]{0,2,1:T(4,128)S(1)}, f32[128,1,4]{0,2,1:T(4,128)S(1)}, s32[16,512]{1,0:T(8,128)S(1)}, s32[128]{0:T(128)S(1)}, /*index=...) while((s32[]{:T(128)}, f32[128,1,4]{0,2,1:T(4,128)S(1)}, ...), condition=%wide.region_4.5_spmd.clone, body=%wide.region_1.4_spmd.clone.sunk | while | flops 68749824 | bytes 2589804 | solution.py:134
  306.1 964.0 %while.47 = (s32[]{:T(128)}, bf16[128,128]{1,0:T(8,128)(2,1)S(1)}, bf16[128,128]{1,0:T(8,128)(2,1)S(1)}, f32[128,256]{0,1:T(8,128)S(1)}, f32[128,1,4,128]{3,0,2,...) while((s32[]{:T(128)}, bf16[128,128]{1,0:T(8,128)(2,1)S(1)}, ...), condition=%wide.region_7.8_spmd.clone, body=%wide.region_6.7_spmd.clone.sunk | while | flops 84688912 | bytes 3808750 | solution.py:151
  317.1 4.5 collective-permute-done.2
  332.5 4.0 collective-permute-done.2
  347.3 4.0 collective-permute-done.2
  362.1 4.5 collective-permute-done.2
  377.3 4.3 collective-permute-done.2
  392.5 4.6 collective-permute-done.2
  407.9 4.0 collective-permute-done.2
  422.7 4.0 collective-permute-done.2
  437.5 4.0 collective-permute-done.2
  452.3 4.0 collective-permute-done.2
  467.1 4.0 collective-permute-done.2
  496.7 4.0 collective-permute-done.2
  511.5 4.7 collective-permute-done.2
  526.9 5.3 collective-permute-done.2
  543.0 4.4 collective-permute-done.2
  573.0 4.3 collective-permute-done.2
  588.2 4.5 collective-permute-done.2
  603.5 4.1 collective-permute-done.2
  618.5 4.4 collective-permute-done.2
  633.7 4.0 collective-permute-done.2
  648.5 4.0 collective-permute-done.2
  663.3 4.0 collective-permute-done.2
  678.1 4.0 collective-permute-done.2
  692.9 4.0 collective-permute-done.2
  722.5 4.0 collective-permute-done.2
  737.3 4.7 collective-permute-done.2
  752.7 5.3 collective-permute-done.2
  768.8 4.4 collective-permute-done.2
  798.8 4.3 collective-permute-done.2
  814.0 4.5 collective-permute-done.2
  829.3 4.1 collective-permute-done.2
  844.3 4.4 collective-permute-done.2
  859.5 4.0 collective-permute-done.2
  874.3 4.0 collective-permute-done.2
  889.1 4.0 collective-permute-done.2
  963.1 4.7 collective-permute-done.2
  978.5 5.3 collective-permute-done.2
  994.6 4.4 collective-permute-done.2
  1024.6 4.3 collective-permute-done.2
  1039.8 4.5 collective-permute-done.2
  1055.1 4.1 collective-permute-done.2
  1070.1 4.4 collective-permute-done.2
  1129.7 4.0 collective-permute-done.2
  1144.5 4.0 collective-permute-done.2
  1188.8 4.7 collective-permute-done.2
  1204.3 5.3 collective-permute-done.2
  1220.4 4.4 collective-permute-done.2
  1250.4 4.3 collective-permute-done.2
  1265.6 4.5 collective-permute-done.2
  1270.8 129.4 %all_to_all.138 = bf16[8,16,128]{2,1,0:T(8,128)(2,1)S(1)} all-to-all(bf16[8,16,128]{2,1,0:T(8,128)(2,1)S(1)} %bitcast.229), channel_id=1, replica_groups=mesh['ctx'=64,'head'=8] {'head'}, dimensions={0} | all-to-all | bytes 65536 | tf_op jit(solution)/shard_map/all_to_all | solution.py:161
  1400.2 4.0 all-to-all-start.6
  1405.1 6.3 all-to-all-done.6
  1411.4 4.0 all-to-all-start.5
  1416.6 6.8 all-to-all-done.5
  (1131 shorter events, 787.5 us)
Async XLA Ops:
  7.2 272.4 %all-gather.2.cloned.1.call-start = ((), (), s32[]{:S(2)}) async-start(), calls=%async_computation.8 | async-start | bytes 2129920 | tf_op jit(solution)/shard_map/all_gather | solution.py:130
  28.5 12.1 all-to-all-start.2
  40.6 13.7 all-to-all-start.3
  54.3 13.5 all-to-all-start.4
  67.8 238.3 %all-to-all-start.1 = ((bf16[16,8,128]{2,0,1:T(8,128)(2,1)}), bf16[16,8,128]{2,0,1:T(8,128)(2,1)S(1)}, u32[]{:S(2)}, u32[]{:S(2)}) async-start(bf16[16,8,128]{2,0,1:T(8,128)(2,1)} %copy_bitcast_fusion.5), calls=%async_computation.1 | async-start | bytes 65536 | tf_op jit(solution)/shard_map/all_to_all | solution.py:39
  311.5 10.1 collective-permute-start.2
  326.5 9.9 collective-permute-start.2
  341.3 9.9 collective-permute-start.2
  356.1 10.4 collective-permute-start.2
  371.4 10.3 collective-permute-start.2
  386.5 10.5 collective-permute-start.2
  401.9 9.9 collective-permute-start.2
  416.7 9.9 collective-permute-start.2
  431.5 9.9 collective-permute-start.2
  446.3 9.9 collective-permute-start.2
  461.1 9.9 collective-permute-start.2
  475.9 9.9 collective-permute-start.2
  505.5 10.6 collective-permute-start.2
  521.0 11.2 collective-permute-start.2
  537.1 10.4 collective-permute-start.2
  552.3 9.9 collective-permute-start.2
  567.1 10.3 collective-permute-start.2
  582.2 10.5 collective-permute-start.2
  597.6 10.1 collective-permute-start.2
  612.5 10.3 collective-permute-start.2
  627.7 9.9 collective-permute-start.2
  642.5 9.9 collective-permute-start.2
  657.3 9.9 collective-permute-start.2
  672.1 9.9 collective-permute-start.2
  686.9 9.9 collective-permute-start.2
  731.3 10.6 collective-permute-start.2
  746.8 11.2 collective-permute-start.2
  762.9 10.4 collective-permute-start.2
  778.1 9.9 collective-permute-start.2
  792.9 10.3 collective-permute-start.2
  808.0 10.5 collective-permute-start.2
  823.4 10.1 collective-permute-start.2
  838.3 10.3 collective-permute-start.2
  853.5 9.9 collective-permute-start.2
  868.3 9.9 collective-permute-start.2
  897.9 9.9 collective-permute-start.2
  912.7 9.9 collective-permute-start.2
  957.1 10.6 collective-permute-start.2
  972.6 11.2 collective-permute-start.2
  988.7 10.4 collective-permute-start.2
  1003.9 9.9 collective-permute-start.2
  1018.7 10.3 collective-permute-start.2
  1033.8 10.5 collective-permute-start.2
  1049.2 10.1 collective-permute-start.2
  1064.1 10.3 collective-permute-start.2
  1079.3 9.9 collective-permute-start.2
  1094.1 9.9 collective-permute-start.2
  1123.7 9.9 collective-permute-start.2
  1138.5 9.9 collective-permute-start.2
  1153.3 9.9 collective-permute-start.2
  1168.1 9.9 collective-permute-start.2
  1182.9 10.6 collective-permute-start.2
  1198.4 11.2 collective-permute-start.2
  1214.5 10.4 collective-permute-start.2
  1229.7 9.9 collective-permute-start.2
  1244.5 10.3 collective-permute-start.2
  1259.6 10.5 collective-permute-start.2
  1400.2 11.2 all-to-all-start.6
  1411.4 12.0 all-to-all-start.5
  (138 other events, 1294.7 us)
Sparse Core Ops, SparseCore 0:
  27.1 252.4 all-gather.1
where the time goes:
time: 1440 us; the launch traced here: 1430 us
  waiting for transfers between devices  750 us (52%)
  starting transfers between devices  394 us (27%)
  blocking collectives  148 us (10%)
  matrix products  83.2 us (6%)
  other arithmetic  16.6 us (1%)
  local copies, waits for them, and re-layouts  15.7 us (1%)
    ppermute x192, waiting for transfers between devices, shifted(): lax.ppermute(array, axis, [(i, (i + by) % size) for i in range(size)])  512 us
    ppermute x192, starting transfers between devices, shifted(): lax.ppermute(array, axis, [(i, (i + by) % size) for i in range(size)])  369 us
    all_gather x1, waiting for transfers between devices, on_device(): portion = lax.all_gather(key_loc, 'ctx', axis=0, tiled=True)  207 us
    all_to_all x1, blocking collectives, on_device(): lax.all_to_all(value_part, 'head', split_axis=0, concat_axis=1, tiled=True)  129 us
    dot_general x80, matrix products, scores_of(): jnp.einsum('rcgd,ncd->rcgn', heads_of_queries, key_split, preferred_eleme...  31.8 us
  transfers between devices with their start and end apart: 199, of which 198 were waited for; matrix products, arithmetic and copies ran while one was open for 8% of the time, Pallas kernels for 0%

commit v1 on v0

--- a/solution.py
+++ b/solution.py
@@ -127,7 +127,9 @@
     query_zero = jnp.zeros((row_count, kv_local, group_width, HEAD_WIDTH), jnp.float32)
     pair_zero = jnp.zeros((row_count, 2 * kv_local * HEAD_WIDTH), jnp.float32)
     running = stats_start
-    portion = lax.all_gather(key_loc, "ctx", axis=0, tiled=True)
+    portion = jnp.concatenate(
+        lax.all_to_all(jnp.stack([key_loc] * lax.axis_size("ctx")), "ctx", 0, 0), axis=0
+    )
     length = portion.shape[0]
     block_len, block_count = block_split(length)
     key_pos = all_positions

time: 1440 us -> 1230 us (0.85)
  waiting for transfers between devices: 750 us -> 587 us
  blocking collectives: 148 us -> 93.7 us
  starting transfers between devices: 394 us -> 419 us
    all_gather x1 -> x0, waiting for transfers between devices: 207 us -> none  [on_device(): portion = lax.all_gather(key_loc, 'ctx', axis=0, tiled=True)]
    all_to_all x1, blocking collectives: 129 us -> 81.9 us  [on_device(): lax.all_to_all(value_part, 'head', split_axis=0, concat_axis=1, tiled=True)]
    all_to_all x1 -> x2, waiting for transfers between devices: 7.53 us -> 48.2 us  [the longest x1 42.5 us: on_device(): lax.all_to_all(jnp.stack([key_loc] * lax.axis_size('ctx')), 'ctx', 0, 0)]
    all_to_all x1 -> x2, starting transfers between devices: 4.36 us -> 23 us  [the longest x1 11.8 us: on_device(): lax.all_to_all(keys, 'head', split_axis=1, concat_axis=0, tiled=True)]
  transfers between devices with their start and end apart: 199 -> 199, of which waited for: 198 -> 197; matrix products, arithmetic and copies ran while one was open for 8% -> 9% of each run, Pallas kernels for 0% -> 0%
where the time goes in v1:
time: 1230 us
  waiting for transfers between devices  587 us (48%)
  starting transfers between devices  419 us (34%)
  blocking collectives  93.7 us (8%)
  matrix products  83.1 us (7%)
  local copies, waits for them, and re-layouts  17.6 us (1%)
  other arithmetic  15.3 us (1%)
    ppermute x192, waiting for transfers between devices, shifted(): lax.ppermute(array, axis, [(i, (i + by) % size) for i in range(size)])  512 us
    ppermute x192, starting transfers between devices, shifted(): lax.ppermute(array, axis, [(i, (i + by) % size) for i in range(size)])  371 us
    all_to_all x1, blocking collectives, on_device(): lax.all_to_all(value_part, 'head', split_axis=0, concat_axis=1, tiled=True)  81.9 us
    all_to_all x1, waiting for transfers between devices, on_device(): lax.all_to_all(jnp.stack([key_loc] * lax.axis_size('ctx')), 'ctx', 0, 0)  42.5 us
    dot_general x80, matrix products, scores_of(): jnp.einsum('rcgd,ncd->rcgn', heads_of_queries, key_split, preferred_eleme...  31.8 us
  transfers between devices with their start and end apart: 199, of which 197 were waited for; matrix products, arithmetic and copies ran while one was open for 9% of the time, Pallas kernels for 0%

profile of v1, /device:TPU:1, one launch (start us, length us, event | category | flops | bytes accessed | tf_op | source)
XLA Modules:
  0.0 1225.1 jit_solution(5955161773192698058)
XLA Ops:
  2.0 11.8 all-to-all-start
  15.4 5.7 all-to-all-done
  21.1 4.0 all-to-all-start.2
  26.7 6.5 all-to-all-done.2
  33.2 5.0 all-to-all-start.4
  39.1 7.3 all-to-all-done.4
  46.4 11.8 all_to_all.142
  60.1 11.2 all-to-all-start.3
  75.4 42.5 %all-to-all-done.3 = bf16[64,128,128]{2,1,0:T(8,128)(2,1)} async-done(((bf16[64,128,128]{2,1,0:T(8,128)(2,1)}), bf16[64,128,128]{2,1,0:T(8,128)(2,1)}, u32[]{:S(2)}, u32[]{:S(2)}) %all-to-all-start.3) | async-done | bytes 2097184 | tf_op jit(solution)/shard_map/all_to_all | solution.py:131
  117.9 8.4 all-to-all-start.1
  126.3 26.5 %while.46 = (s32[]{:T(128)}, f32[128,1,4]{0,2,1:T(4,128)S(1)}, f32[128,1,4]{0,2,1:T(4,128)S(1)}, s32[16,512]{1,0:T(8,128)S(1)}, s32[128]{0:T(128)S(1)}, /*index=...) while((s32[]{:T(128)}, f32[128,1,4]{0,2,1:T(4,128)S(1)}, ...), condition=%wide.region_4.5_spmd.clone, body=%wide.region_1.4_spmd.clone.sunk | while | flops 68749824 | bytes 2589804 | solution.py:136
  152.8 965.8 %while.47 = (s32[]{:T(128)}, bf16[128,128]{1,0:T(8,128)(2,1)S(1)}, bf16[128,128]{1,0:T(8,128)(2,1)S(1)}, f32[128,256]{0,1:T(8,128)S(1)}, f32[128,1,4,128]{3,0,2,...) while((s32[]{:T(128)}, bf16[128,128]{1,0:T(8,128)(2,1)S(1)}, ...), condition=%wide.region_7.8_spmd.clone, body=%wide.region_6.7_spmd.clone.sunk | while | flops 84688912 | bytes 3808750 | solution.py:153
  164.7 5.6 collective-permute-done.2
  196.0 4.3 collective-permute-done.2
  211.1 4.6 collective-permute-done.2
  226.5 4.0 collective-permute-done.2
  241.3 4.3 collective-permute-done.2
  256.5 4.0 collective-permute-done.2
  271.3 4.0 collective-permute-done.2
  286.1 4.0 collective-permute-done.2
  300.9 4.0 collective-permute-done.2
  315.7 4.0 collective-permute-done.2
  345.2 4.0 collective-permute-done.2
  360.0 4.7 collective-permute-done.2
  375.5 5.3 collective-permute-done.2
  391.6 4.4 collective-permute-done.2
  421.6 4.3 collective-permute-done.2
  436.8 4.5 collective-permute-done.2
  452.1 4.1 collective-permute-done.2
  467.1 4.4 collective-permute-done.2
  482.2 4.0 collective-permute-done.2
  511.8 4.0 collective-permute-done.2
  571.0 4.0 collective-permute-done.2
  585.8 4.7 collective-permute-done.2
  601.3 5.3 collective-permute-done.2
  617.4 4.4 collective-permute-done.2
  647.4 4.3 collective-permute-done.2
  662.5 4.5 collective-permute-done.2
  677.9 4.1 collective-permute-done.2
  692.8 4.4 collective-permute-done.2
  722.8 4.0 collective-permute-done.2
  737.6 4.0 collective-permute-done.2
  767.2 4.0 collective-permute-done.2
  796.8 4.0 collective-permute-done.2
  811.6 4.7 collective-permute-done.2
  827.1 5.3 collective-permute-done.2
  843.2 4.4 collective-permute-done.2
  873.2 4.3 collective-permute-done.2
  888.3 4.5 collective-permute-done.2
  903.7 4.1 collective-permute-done.2
  918.6 4.4 collective-permute-done.2
  933.8 4.0 collective-permute-done.2
  948.6 4.0 collective-permute-done.2
  993.0 4.0 collective-permute-done.2
  1022.6 4.0 collective-permute-done.2
  1037.4 4.7 collective-permute-done.2
  1052.9 5.3 collective-permute-done.2
  1069.0 4.4 collective-permute-done.2
  1099.0 4.3 collective-permute-done.2
  1114.1 4.5 collective-permute-done.2
  1119.4 81.9 %all_to_all.143 = bf16[8,16,128]{2,1,0:T(8,128)(2,1)S(1)} all-to-all(bf16[8,16,128]{2,1,0:T(8,128)(2,1)S(1)} %bitcast.229), channel_id=1, replica_groups=mesh['ctx'=64,'head'=8] {'head'}, dimensions={0} | all-to-all | bytes 65536 | tf_op jit(solution)/shard_map/all_to_all | solution.py:163
  1206.1 6.3 all-to-all-done.7
  1212.4 4.0 all-to-all-start.6
  1217.6 6.8 all-to-all-done.6
  (1133 shorter events, 793.5 us)
Async XLA Ops:
  2.0 19.1 %all-to-all-start = ((bf16[16,8,128]{2,0,1:T(8,128)(2,1)}), bf16[16,8,128]{2,0,1:T(8,128)(2,1)S(1)}, u32[]{:S(2)}, u32[]{:S(2)}) async-start(bf16[16,8,128]{2,0,1:T(8,128)(2,1)} %copy_bitcast_fusion.6), calls=%async_computation | async-start | bytes 65536 | tf_op jit(solution)/shard_map/all_to_all | solution.py:38
  21.1 12.1 all-to-all-start.2
  33.2 13.2 %all-to-all-start.4 = ((bf16[16,8,512]{2,0,1:T(8,128)(2,1)}), bf16[16,8,512]{2,0,1:T(8,128)(2,1)S(1)}, u32[]{:S(2)}, u32[]{:S(2)}) async-start(bf16[16,8,512]{2,0,1:T(8,128)(2,1)} %bitcast.157), calls=%async_computation.4 | async-start | bytes 262144 | tf_op jit(solution)/shard_map/all_to_all | solution.py:37
  60.1 57.8 %all-to-all-start.3 = ((bf16[64,128,128]{2,1,0:T(8,128)(2,1)}), bf16[64,128,128]{2,1,0:T(8,128)(2,1)}, u32[]{:S(2)}, u32[]{:S(2)}) async-start(bf16[64,128,128]{2,1,0:T(8,128)(2,1)} %stack.2), calls=%async_computation.3 | async-start | bytes 4194304 | tf_op jit(solution)/shard_map/all_to_all | solution.py:131
  117.9 34.9 %all-to-all-start.1 = ((bf16[16,8,128]{2,0,1:T(8,128)(2,1)}), bf16[16,8,128]{2,0,1:T(8,128)(2,1)S(1)}, u32[]{:S(2)}, u32[]{:S(2)}) async-start(bf16[16,8,128]{2,0,1:T(8,128)(2,1)} %copy_bitcast_fusion.5), calls=%async_computation.1 | async-start | bytes 65536 | tf_op jit(solution)/shard_map/all_to_all | solution.py:39
  159.9 10.5 collective-permute-start.2
  190.0 10.3 collective-permute-start.2
  205.2 10.5 collective-permute-start.2
  220.6 9.9 collective-permute-start.2
  235.4 10.3 collective-permute-start.2
  250.5 9.9 collective-permute-start.2
  265.3 9.9 collective-permute-start.2
  280.1 9.9 collective-permute-start.2
  294.9 9.9 collective-permute-start.2
  309.7 9.9 collective-permute-start.2
  324.5 9.9 collective-permute-start.2
  339.3 9.9 collective-permute-start.2
  354.1 10.6 collective-permute-start.2
  369.6 11.2 collective-permute-start.2
  385.7 10.4 collective-permute-start.2
  415.7 10.3 collective-permute-start.2
  430.8 10.5 collective-permute-start.2
  446.2 10.1 collective-permute-start.2
  461.1 10.3 collective-permute-start.2
  476.3 9.9 collective-permute-start.2
  505.9 9.9 collective-permute-start.2
  520.7 9.9 collective-permute-start.2
  550.3 9.9 collective-permute-start.2
  565.1 9.9 collective-permute-start.2
  579.9 10.6 collective-permute-start.2
  595.4 11.2 collective-permute-start.2
  611.4 10.3 collective-permute-start.2
  626.6 9.9 collective-permute-start.2
  641.4 10.3 collective-permute-start.2
  656.6 10.5 collective-permute-start.2
  671.9 10.1 collective-permute-start.2
  686.9 10.3 collective-permute-start.2
  702.1 9.9 collective-permute-start.2
  716.9 9.9 collective-permute-start.2
  731.7 9.9 collective-permute-start.2
  746.5 9.9 collective-permute-start.2
  761.3 9.9 collective-permute-start.2
  776.1 9.9 collective-permute-start.2
  790.9 9.9 collective-permute-start.2
  805.7 10.6 collective-permute-start.2
  821.1 11.2 collective-permute-start.2
  837.2 10.4 collective-permute-start.2
  867.2 10.3 collective-permute-start.2
  882.4 10.5 collective-permute-start.2
  897.7 10.1 collective-permute-start.2
  912.7 10.3 collective-permute-start.2
  927.9 9.9 collective-permute-start.2
  942.7 9.9 collective-permute-start.2
  957.5 9.9 collective-permute-start.2
  972.3 9.9 collective-permute-start.2
  1016.7 9.9 collective-permute-start.2
  1031.5 10.6 collective-permute-start.2
  1046.9 11.2 collective-permute-start.2
  1063.0 10.3 collective-permute-start.2
  1078.2 9.9 collective-permute-start.2
  1093.0 10.3 collective-permute-start.2
  1108.2 10.5 collective-permute-start.2
  1201.3 11.1 all-to-all-start.7
  1212.4 12.0 all-to-all-start.6
  (139 other events, 1256.5 us)
